TPU v7x, 256 devices: a whole 4x4x8 slice. The times are simulated.
256 devices in a mesh: dp: 128 (over y, z, x), rep: 2 (over core).
Axes of the slice: x: 4, y: 4, z: 8, core: 2. Of those that a mesh axis runs over, the one named last changes fastest.
Arguments:
- embeddings: float32 [131072, 1024], P(('dp', 'rep')), may hold values from -6 to 6
- cluster_ids: int32 [131072, 1], P(('dp', 'rep')), may hold values from 0 to 255; in each aligned block of 512 rows (0 to 511, 512 to 1023, ...) at most 4 rows name the same one
- boundary_slots: int32 [256, 2, 256], P(('dp', 'rep')), may hold values from 0 to 1023
Outputs:
- member_max: float32 [256, 1024], P(('dp', 'rep'))
- centrality: float32 [256, 1024], P(('dp', 'rep'))
Inputs may be any that keep to these rules, and one draw needn't show every extreme that they name: `cluster_ids`: among the rows of one device, at most 4 name the same cluster, a bound that some block reaches of them; every cluster is named by some row.
All inputs are finite; a program needn't handle non-finite values.
Results may differ from a plain program's by a relative error of at most 0.0024.
Values may be sent and summed in bfloat16 or wider, within the bound.
A program may use at most 64 MiB of HBM per device.

v0:
```python
import jax
import jax.numpy as jnp
from jax import lax
from jax.sharding import PartitionSpec as P

SLOTS = 1024
eps = 1e-06


def from_behind(array, axis, by):
    peers = lax.axis_size(axis)
    pairs = [(i, i + by) for i in range(peers) if 0 <= i + by < peers]
    return lax.ppermute(array, axis, pairs)


def per_device(embeddings, cluster_ids, boundary_slots):
    n_chips = lax.axis_size("dp")
    n_cores = lax.axis_size("rep")
    owners = n_chips * n_cores
    width = embeddings.shape[1]
    slots = SLOTS
    capacity = slots // owners
    bound = boundary_slots.shape[2]
    me = lax.axis_index(("dp", "rep"))
    labels = cluster_ids[:, 0]
    member_of = labels[:, None] == jnp.arange(owners, dtype=jnp.int32)[None, :]
    running = jnp.cumsum(member_of.astype(jnp.int32), axis=0)
    ranks = jnp.sum(jnp.where(member_of, running, 0), axis=1) - 1
    targets = labels * capacity + ranks
    unit_full = embeddings * lax.rsqrt(
        jnp.sum(embeddings * embeddings, axis=1, keepdims=True) + eps
    )
    unit_half = unit_full.astype(jnp.bfloat16)
    outgoing = jnp.zeros((slots, width), jnp.bfloat16).at[targets].set(unit_half)
    member_half = member_of.astype(jnp.bfloat16)
    shaped = outgoing.reshape(n_chips, n_cores, capacity, width)
    arrived = lax.all_to_all(
        lax.all_to_all(shaped, "dp", split_axis=0, concat_axis=0, tiled=True),
        "rep",
        split_axis=1,
        concat_axis=1,
        tiled=True,
    )
    members = arrived.reshape(slots, width)
    partial_sums = lax.dot_general(
        member_half, unit_half, (((0,), (0,)), ((), ())), preferred_element_type=jnp.float32
    )
    total = lax.psum(partial_sums, ("dp", "rep"))
    own_sum = lax.dynamic_slice_in_dim(total, me, 1, 0)
    direction = own_sum[0] * lax.rsqrt(jnp.sum(own_sum * own_sum) + eps)
    lengths = jnp.einsum("se,se->s", members, members, preferred_element_type=jnp.float32)
    filled = lengths > 0.5
    filled_int = filled.astype(jnp.int32)
    count = jnp.sum(filled_int)
    order = jnp.argsort(1 - filled_int, stable=True)
    picks = boundary_slots[0] % count
    positions = order[picks.reshape(-1)]
    outward = members[positions]
    lower = from_behind(outward[bound:], ("dp", "rep"), 1)
    upper = from_behind(outward[:bound], ("dp", "rep"), -1)
    candidates = jnp.concatenate([members, lower, upper], axis=0)
    cand_ok = jnp.concatenate(
        [filled, jnp.full((bound,), me > 0), jnp.full((bound,), me < owners - 1)]
    )
    column = jnp.arange(slots + 2 * bound, dtype=jnp.int32)
    block = min(512, slots)

    def one_block(start):
        block_rows = lax.dynamic_slice_in_dim(members, start, block, 0)
        scores = lax.dot_general(
            block_rows, candidates, (((1,), (1,)), ((), ())), preferred_element_type=jnp.float32
        )
        row_pos = start + jnp.arange(block, dtype=jnp.int32)
        keep = cand_ok[None, :] & (column[None, :] != row_pos[:, None])
        return jnp.max(jnp.where(keep, scores, -1.0), axis=1)

    starts = jnp.arange(slots // block, dtype=jnp.int32) * block
    best = lax.map(one_block, starts).reshape(slots)
    member_max = jnp.where(filled, best, 0.0)
    central = jnp.dot(
        members, direction, precision=lax.Precision.HIGHEST, preferred_element_type=jnp.float32
    )
    centrality = jnp.where(filled, central, 0.0)
    return (member_max[None, :], centrality[None, :])


def solution(mesh):
    placed = (P(("dp", "rep"), None), P(("dp", "rep"), None), P(("dp", "rep"), None, None))
    return jax.shard_map(
        per_device,
        mesh=mesh,
        in_specs=placed,
        out_specs=(P(("dp", "rep"), None), P(("dp", "rep"), None)),
        check_vma=False,
    )
```

profile of v0, /device:TPU:8, one launch (start us, length us, event | category | flops | bytes accessed | tf_op | source)
XLA Modules:
  0.0 374.8 jit_solution(14825172263603566123)
XLA Ops:
  7.2 1.8 multiply_reduce_fusion
  10.6 4.2 %scatter_custom_fusion = bf16[1024,1024]{1,0:T(8,128)(2,1)} fusion(s32[512]{0:T(512)S(1)} %bitcast.58, bf16[]{:T(256)} %constant.27.clone.1, f32[512,1024]{1,0:T(8,128)S(1)} %copy-done, f32[512]{0:T(512)S(1)} %add_rsqrt_fusion), kind=kCustom, calls=%fused_computation.16 | custom fusion | flops 1048576 | bytes 4196354 | tf_op jit(solution)/shard_map/scatter | solution.py:34
  14.7 4.1 %reshape.106 = bf16[128,2,4,1024]{3,2,1,0:T(4,128)(2,1)} reshape(bf16[1024,1024]{1,0:T(8,128)(2,1)} %scatter_custom_fusion) | data formatting | bytes 4194304 | tf_op jit(solution)/shard_map/reshape | solution.py:36
  18.8 15.9 %all-to-all-start = ((bf16[128,2,4,1024]{3,2,1,0:T(4,128)(2,1)}), bf16[128,2,4,1024]{3,2,1,0:T(4,128)(2,1)}, u32[]{:S(2)}, u32[]{:S(2)}) async-start(bf16[128,2,4,1024]{3,2,1,0:T(4,128)(2,1)} %reshape.106), calls=%async_computation | async-start | bytes 4194304 | tf_op jit(solution)/shard_map/all_to_all | solution.py:38
  34.8 1.7 fusion.12
  36.5 268.0 %all-reduce.2.cloned.1.call-done = f32[256,1024]{1,0:T(8,128)} async-done(((f32[256,1024]{1,0:T(8,128)}), f32[256,1024]{1,0:T(8,128)}) %all-reduce.2.cloned.1.call-update) | async-done | bytes 1048592 | tf_op jit(solution)/shard_map/psum | solution.py:48
  304.5 1.4 multiply_reduce_fusion.1
  306.6 2.3 copy.14
  308.9 5.4 %all_to_all.10 = bf16[128,2,4,1024]{3,2,0,1:T(4,128)(2,1)S(1)} all-to-all(bf16[128,2,4,1024]{3,2,0,1:T(4,128)(2,1)S(1)} %copy.14), channel_id=1, replica_groups=mesh['dp'=128,'rep'=2] {'rep'}, dimensions={1} | all-to-all | bytes 4194304 | tf_op jit(solution)/shard_map/all_to_all | solution.py:37
  314.3 2.6 copy.15
  317.0 2.5 reshape.107
  320.0 2.5 fusion.15
  325.2 4.4 %sort.17 = (s32[1024]{0:T(1024)}, s32[1024]{0:T(1024)S(1)}) sort(s32[1024]{0:T(1024)S(1)} %get-tuple-element.73, s32[1024]{0:T(1024)S(1)} %iota.25), dimensions={0}, to_apply=%region_5.6 | sort | flops 10240 | bytes 16384 | tf_op jit(solution)/shard_map/jit(argsort)/sort | solution.py:55
  329.6 2.3 gather_fusion
  331.9 2.1 gather_fusion.1
  334.0 1.1 fusion.21
  335.0 2.0 collective-permute-start
  337.1 7.7 %collective-permute-start.1 = (bf16[256,1024]{1,0:T(8,128)(2,1)}, bf16[256,1024]{1,0:T(8,128)(2,1)S(1)}, u32[]{:S(2)}, u32[]{:S(2)}) collective-permute-start(bf16[256,1024]{1,0:T(8,128)(2,1)} %get-tuple-element.71), channel_id=1, source_target_pairs={{1,0},{2,1},{3,2},{4,3},{5,4},{6,5},{7,6},{8,7},{9,8},{10,9},{11,1... | collective-permute-start | bytes 1572872 | tf_op jit(solution)/shard_map/ppermute | solution.py:13
  344.9 5.1 %collective-permute-done = bf16[256,1024]{1,0:T(8,128)(2,1)S(1)} collective-permute-done((bf16[256,1024]{1,0:T(8,128)(2,1)}, bf16[256,1024]{1,0:T(8,128)(2,1)S(1)}, u32[]{:S(2)}, u32[]{:S(2)}) %collective-permute-start) | collective-permute-done | bytes 524320 | tf_op jit(solution)/shard_map/ppermute | solution.py:13
  349.9 1.9 collective-permute-done.1
  351.8 1.9 pad_maximum_fusion
  353.7 13.6 %while.11 = (s32[]{:T(128)}, f32[2,512]{1,0:T(2,128)S(1)}, pred[1536]{0:T(1024)(128)(4,1)S(1)}, s32[2]{0:T(128)S(1)}, bf16[1024,1024]{1,0:T(8,128)(2,1)S(1)}, /*...) while((s32[]{:T(128)}, f32[2,512]{1,0:T(2,128)S(1)}, ...), condition=%wide.region_9.10_spmd.clone, body=%wide.region_7.9_spmd.clone.sunk | while | flops 1613758464 | bytes 4206743 | solution.py:78
  356.4 4.0 %fusion.29 = f32[512]{0:T(512)S(1)} fusion(bf16[1536,1024]{1,0:T(8,128)(2,1)} %get-tuple-element.134, s32[512]{0:T(512)S(1)} %iota_add_fusion.2, pred[1536]{0:T(1024)(128)(4,1)S(1)} %get-tuple-element.131, bf16[1024,1024]{1,0:T(8,128)(2,1)S(1)} %get-tuple-element.133, s32[]{:T(128)S(6)} %select_n.90), kind=kOutput, calls=%fused_computation.7.clone.1 | convolution fusion | flops 1613757952 | bytes 4200452 | tf_op jit(solution)/shard_map/while/body/eval_jaxpr/dot_general | solution.py:70
  363.2 4.0 %fusion.29 = f32[512]{0:T(512)S(1)} fusion(bf16[1536,1024]{1,0:T(8,128)(2,1)} %get-tuple-element.134, s32[512]{0:T(512)S(1)} %iota_add_fusion.2, pred[1536]{0:T(1024)(128)(4,1)S(1)} %get-tuple-element.131, bf16[1024,1024]{1,0:T(8,128)(2,1)S(1)} %get-tuple-element.133, s32[]{:T(128)S(6)} %select_n.90), kind=kOutput, calls=%fused_computation.7.clone.1 | convolution fusion | flops 1613757952 | bytes 4200452 | tf_op jit(solution)/shard_map/while/body/eval_jaxpr/dot_general | solution.py:70
  (44 shorter events, 6.4 us)
Async XLA Ops:
  7.2 1.8 copy-start.1
  9.0 1.6 copy-start
  18.8 287.7 %all-to-all-start = ((bf16[128,2,4,1024]{3,2,1,0:T(4,128)(2,1)}), bf16[128,2,4,1024]{3,2,1,0:T(4,128)(2,1)}, u32[]{:S(2)}, u32[]{:S(2)}) async-start(bf16[128,2,4,1024]{3,2,1,0:T(4,128)(2,1)} %reshape.106), calls=%async_computation | async-start | bytes 4194304 | tf_op jit(solution)/shard_map/all_to_all | solution.py:38
  34.8 269.8 %all-reduce.2.cloned.1.call-start = ((), (), s32[]{:S(2)}) async-start(), calls=%async_computation.2 | async-start | bytes 2097152 | tf_op jit(solution)/shard_map/psum | solution.py:48
  319.5 5.5 %copy-start.2 = (s32[1,2,256]{2,1,0:T(2,128)S(1)}, s32[1,2,256]{2,1,0:T(2,128)}, u32[]{:S(2)}) copy-start(s32[1,2,256]{2,1,0:T(2,128)} %param.7) | copy-start | bytes 6148
  335.0 14.9 %collective-permute-start = (bf16[256,1024]{1,0:T(8,128)(2,1)}, bf16[256,1024]{1,0:T(8,128)(2,1)S(1)}, u32[]{:S(2)}, u32[]{:S(2)}) collective-permute-start(bf16[256,1024]{1,0:T(8,128)(2,1)} %get-tuple-element.70), channel_id=1, source_target_pairs={{0,1},{1,2},{2,3},{3,4},{4,5},{5,6},{6,7},{7,8},{8,9},{9,10},{10,1... | collective-permute-start | bytes 1572872 | tf_op jit(solution)/shard_map/ppermute | solution.py:13
  337.1 14.7 %collective-permute-start.1 = (bf16[256,1024]{1,0:T(8,128)(2,1)}, bf16[256,1024]{1,0:T(8,128)(2,1)S(1)}, u32[]{:S(2)}, u32[]{:S(2)}) collective-permute-start(bf16[256,1024]{1,0:T(8,128)(2,1)} %get-tuple-element.71), channel_id=1, source_target_pairs={{1,0},{2,1},{3,2},{4,3},{5,4},{6,5},{7,6},{8,7},{9,8},{10,9},{11,1... | collective-permute-start | bytes 1572872 | tf_op jit(solution)/shard_map/ppermute | solution.py:13
Sparse Core Ops, SparseCore 0:
  41.0 263.4 all-reduce.1
where the time goes:
time: 376 us; the launch traced here: 375 us
  waiting for transfers between devices  275 us (73%)
  starting transfers between devices  25.7 us (7%)
  local copies, waits for them, and re-layouts  19.2 us (5%)
  other arithmetic  17.7 us (5%)
  between operations  16.3 us (4%)
  matrix products  12.1 us (3%)
  blocking collectives  5.42 us (1%)
    psum x1, waiting for transfers between devices, per_device(): total = lax.psum(partial_sums, ('dp', 'rep'))  268 us
    all_to_all x1, starting transfers between devices, per_device(): lax.all_to_all(shaped, 'dp', split_axis=0, concat_axis=0, tiled=True)  15.9 us
    ppermute x2, starting transfers between devices, from_behind(): return lax.ppermute(array, axis, pairs)  9.77 us
    dot_general x2, matrix products, one_block(): lax.dot_general(block_rows, candidates, (((1,), (1,)), ((), ())), preferr...  8.01 us
  transfers between devices with their start and end apart: 4, of which 3 were waited for; matrix products, arithmetic and copies ran while one was open for 1% of the time, Pallas kernels for 0%

commit v1 on v0

--- a/solution.py
+++ b/solution.py
@@ -45,7 +45,7 @@
     partial_sums = lax.dot_general(
         member_half, unit_half, (((0,), (0,)), ((), ())), preferred_element_type=jnp.float32
     )
-    total = lax.psum(partial_sums, ("dp", "rep"))
+    total = lax.psum(lax.psum(partial_sums, "rep"), "dp")
     own_sum = lax.dynamic_slice_in_dim(total, me, 1, 0)
     direction = own_sum[0] * lax.rsqrt(jnp.sum(own_sum * own_sum) + eps)
     lengths = jnp.einsum("se,se->s", members, members, preferred_element_type=jnp.float32)

time: 376 us -> 369 us (0.981)
  waiting for transfers between devices: 275 us -> 269 us
    psum x1 -> x2, waiting for transfers between devices: 268 us -> 262 us  [per_device(): total = lax.psum(lax.psum(partial_sums, 'rep'), 'dp')]
  transfers between devices with their start and end apart: 4 -> 5, of which waited for: 3 -> 4; matrix products, arithmetic and copies ran while one was open for 1% -> 1% of each run, Pallas kernels for 0% -> 0%
where the time goes in v1:
time: 369 us; the launch traced here: 368 us
  waiting for transfers between devices  269 us (73%)
  starting transfers between devices  25.8 us (7%)
  local copies, waits for them, and re-layouts  19.2 us (5%)
  other arithmetic  17.7 us (5%)
  between operations  16.3 us (4%)
  matrix products  12.1 us (3%)
  blocking collectives  5.42 us (1%)
    psum x2, waiting for transfers between devices, per_device(): total = lax.psum(lax.psum(partial_sums, 'rep'), 'dp')  262 us
    all_to_all x1, starting transfers between devices, per_device(): lax.all_to_all(shaped, 'dp', split_axis=0, concat_axis=0, tiled=True)  15.9 us
    ppermute x2, starting transfers between devices, from_behind(): return lax.ppermute(array, axis, pairs)  9.77 us
    dot_general x2, matrix products, one_block(): lax.dot_general(block_rows, candidates, (((1,), (1,)), ((), ())), preferr...  8.01 us
  transfers between devices with their start and end apart: 5, of which 4 were waited for; matrix products, arithmetic and copies ran while one was open for 1% of the time, Pallas kernels for 0%

profile of v1, /device:TPU:8, one launch (start us, length us, event | category | flops | bytes accessed | tf_op | source)
XLA Modules:
  0.0 368.4 jit_solution(14661034710195251544)
XLA Ops:
  7.2 1.8 multiply_reduce_fusion
  10.6 4.2 %scatter_custom_fusion = bf16[1024,1024]{1,0:T(8,128)(2,1)} fusion(s32[512]{0:T(512)S(1)} %bitcast.58, bf16[]{:T(256)} %constant.27.clone.1, f32[512,1024]{1,0:T(8,128)S(1)} %copy-done, f32[512]{0:T(512)S(1)} %add_rsqrt_fusion), kind=kCustom, calls=%fused_computation.16 | custom fusion | flops 1048576 | bytes 4196354 | tf_op jit(solution)/shard_map/scatter | solution.py:34
  14.7 4.1 %reshape.106 = bf16[128,2,4,1024]{3,2,1,0:T(4,128)(2,1)} reshape(bf16[1024,1024]{1,0:T(8,128)(2,1)} %scatter_custom_fusion) | data formatting | bytes 4194304 | tf_op jit(solution)/shard_map/reshape | solution.py:36
  18.8 15.9 %all-to-all-start = ((bf16[128,2,4,1024]{3,2,1,0:T(4,128)(2,1)}), bf16[128,2,4,1024]{3,2,1,0:T(4,128)(2,1)}, u32[]{:S(2)}, u32[]{:S(2)}) async-start(bf16[128,2,4,1024]{3,2,1,0:T(4,128)(2,1)} %reshape.106), calls=%async_computation | async-start | bytes 4194304 | tf_op jit(solution)/shard_map/all_to_all | solution.py:38
  34.8 1.6 fusion.12
  36.5 33.4 %all-reduce.3.cloned.1.call-done = f32[256,1024]{1,0:T(8,128)} async-done(((f32[256,1024]{1,0:T(8,128)}), f32[256,1024]{1,0:T(8,128)}) %all-reduce.3.cloned.1.call-update) | async-done | bytes 1048592 | tf_op jit(solution)/shard_map/psum | solution.py:48
  69.9 228.3 %all-reduce.5.cloned.1.call-done = f32[256,1024]{1,0:T(8,128)} async-done(((f32[256,1024]{1,0:T(8,128)}), f32[256,1024]{1,0:T(8,128)}) %all-reduce.5.cloned.1.call-update) | async-done | bytes 1048592 | tf_op jit(solution)/shard_map/psum | solution.py:48
  298.2 1.4 multiply_reduce_fusion.1
  300.3 2.3 copy.14
  302.6 5.4 %all_to_all.10 = bf16[128,2,4,1024]{3,2,0,1:T(4,128)(2,1)S(1)} all-to-all(bf16[128,2,4,1024]{3,2,0,1:T(4,128)(2,1)S(1)} %copy.14), channel_id=1, replica_groups=mesh['dp'=128,'rep'=2] {'rep'}, dimensions={1} | all-to-all | bytes 4194304 | tf_op jit(solution)/shard_map/all_to_all | solution.py:37
  308.0 2.6 copy.15
  310.7 2.5 reshape.107
  313.7 2.5 fusion.15
  318.9 4.4 %sort.17 = (s32[1024]{0:T(1024)}, s32[1024]{0:T(1024)S(1)}) sort(s32[1024]{0:T(1024)S(1)} %get-tuple-element.73, s32[1024]{0:T(1024)S(1)} %iota.25), dimensions={0}, to_apply=%region_5.6 | sort | flops 10240 | bytes 16384 | tf_op jit(solution)/shard_map/jit(argsort)/sort | solution.py:55
  323.3 2.3 gather_fusion
  325.6 2.1 gather_fusion.1
  328.7 2.0 collective-permute-start
  330.8 7.7 %collective-permute-start.1 = (bf16[256,1024]{1,0:T(8,128)(2,1)}, bf16[256,1024]{1,0:T(8,128)(2,1)S(1)}, u32[]{:S(2)}, u32[]{:S(2)}) collective-permute-start(bf16[256,1024]{1,0:T(8,128)(2,1)} %get-tuple-element.71), channel_id=1, source_target_pairs={{1,0},{2,1},{3,2},{4,3},{5,4},{6,5},{7,6},{8,7},{9,8},{10,9},{11,1... | collective-permute-start | bytes 1572872 | tf_op jit(solution)/shard_map/ppermute | solution.py:13
  338.6 5.1 %collective-permute-done = bf16[256,1024]{1,0:T(8,128)(2,1)S(1)} collective-permute-done((bf16[256,1024]{1,0:T(8,128)(2,1)}, bf16[256,1024]{1,0:T(8,128)(2,1)S(1)}, u32[]{:S(2)}, u32[]{:S(2)}) %collective-permute-start) | collective-permute-done | bytes 524320 | tf_op jit(solution)/shard_map/ppermute | solution.py:13
  343.6 1.9 collective-permute-done.1
  345.5 1.9 pad_maximum_fusion
  347.4 13.6 %while.11 = (s32[]{:T(128)}, f32[2,512]{1,0:T(2,128)S(1)}, pred[1536]{0:T(1024)(128)(4,1)S(1)}, s32[2]{0:T(128)S(1)}, bf16[1024,1024]{1,0:T(8,128)(2,1)S(1)}, /*...) while((s32[]{:T(128)}, f32[2,512]{1,0:T(2,128)S(1)}, ...), condition=%wide.region_9.10_spmd.clone, body=%wide.region_7.9_spmd.clone.sunk | while | flops 1613758464 | bytes 4206743 | solution.py:78
  350.1 4.0 %fusion.29 = f32[512]{0:T(512)S(1)} fusion(bf16[1536,1024]{1,0:T(8,128)(2,1)} %get-tuple-element.134, s32[512]{0:T(512)S(1)} %iota_add_fusion.2, pred[1536]{0:T(1024)(128)(4,1)S(1)} %get-tuple-element.131, bf16[1024,1024]{1,0:T(8,128)(2,1)S(1)} %get-tuple-element.133, s32[]{:T(128)S(6)} %select_n.90), kind=kOutput, calls=%fused_computation.7.clone.1 | convolution fusion | flops 1613757952 | bytes 4200452 | tf_op jit(solution)/shard_map/while/body/eval_jaxpr/dot_general | solution.py:70
  356.9 4.0 %fusion.29 = f32[512]{0:T(512)S(1)} fusion(bf16[1536,1024]{1,0:T(8,128)(2,1)} %get-tuple-element.134, s32[512]{0:T(512)S(1)} %iota_add_fusion.2, pred[1536]{0:T(1024)(128)(4,1)S(1)} %get-tuple-element.131, bf16[1024,1024]{1,0:T(8,128)(2,1)S(1)} %get-tuple-element.133, s32[]{:T(128)S(6)} %select_n.90), kind=kOutput, calls=%fused_computation.7.clone.1 | convolution fusion | flops 1613757952 | bytes 4200452 | tf_op jit(solution)/shard_map/while/body/eval_jaxpr/dot_general | solution.py:70
  (47 shorter events, 7.5 us)
Async XLA Ops:
  7.2 1.8 copy-start.1
  9.0 1.6 copy-start
  18.8 281.4 %all-to-all-start = ((bf16[128,2,4,1024]{3,2,1,0:T(4,128)(2,1)}), bf16[128,2,4,1024]{3,2,1,0:T(4,128)(2,1)}, u32[]{:S(2)}, u32[]{:S(2)}) async-start(bf16[128,2,4,1024]{3,2,1,0:T(4,128)(2,1)} %reshape.106), calls=%async_computation | async-start | bytes 4194304 | tf_op jit(solution)/shard_map/all_to_all | solution.py:38
  34.8 35.1 %all-reduce.3.cloned.1.call-start = ((), (), s32[]{:S(2)}) async-start(), calls=%async_computation.2 | async-start | bytes 2097152 | tf_op jit(solution)/shard_map/psum | solution.py:48
  36.4 261.8 %all-reduce.5.cloned.1.call-start = ((), (), s32[]{:S(2)}) async-start(), calls=%async_computation.3 | async-start | bytes 2097152 | tf_op jit(solution)/shard_map/psum | solution.py:48
  313.2 5.5 %copy-start.2 = (s32[1,2,256]{2,1,0:T(2,128)S(1)}, s32[1,2,256]{2,1,0:T(2,128)}, u32[]{:S(2)}) copy-start(s32[1,2,256]{2,1,0:T(2,128)} %param.7) | copy-start | bytes 6148
  328.7 14.9 %collective-permute-start = (bf16[256,1024]{1,0:T(8,128)(2,1)}, bf16[256,1024]{1,0:T(8,128)(2,1)S(1)}, u32[]{:S(2)}, u32[]{:S(2)}) collective-permute-start(bf16[256,1024]{1,0:T(8,128)(2,1)} %get-tuple-element.70), channel_id=1, source_target_pairs={{0,1},{1,2},{2,3},{3,4},{4,5},{5,6},{6,7},{7,8},{8,9},{9,10},{10,1... | collective-permute-start | bytes 1572872 | tf_op jit(solution)/shard_map/ppermute | solution.py:13
  330.8 14.7 %collective-permute-start.1 = (bf16[256,1024]{1,0:T(8,128)(2,1)}, bf16[256,1024]{1,0:T(8,128)(2,1)S(1)}, u32[]{:S(2)}, u32[]{:S(2)}) collective-permute-start(bf16[256,1024]{1,0:T(8,128)(2,1)} %get-tuple-element.71), channel_id=1, source_target_pairs={{1,0},{2,1},{3,2},{4,3},{5,4},{6,5},{7,6},{8,7},{9,8},{10,9},{11,1... | collective-permute-start | bytes 1572872 | tf_op jit(solution)/shard_map/ppermute | solution.py:13
Sparse Core Ops, SparseCore 0:
  38.2 31.6 all-reduce.2
  76.1 222.1 all-reduce.4
